TPU v7x, 32 devices: a whole 2x2x4 slice. The times are simulated.
32 devices in a mesh: slab: 2 (over x), line: 8 (over z, y), band: 2 (over core).
Axes of the slice: x: 2, y: 2, z: 4, core: 2. Of those that a mesh axis runs over, the one named last changes fastest.
Arguments:
- cube: bfloat16 [230, 2048, 256], P('band', ('slab', 'line')), parts along dimension 1, may hold values from -6 to 6
- observed: bfloat16 [13, 2048, 256], P(None, ('slab', 'line')), parts along dimension 1, may hold values from -6 to 6
- along_kernels: bfloat16 [3, 128, 128], replicated, may hold values from -0.3125 to 0.3125
- along_offsets: int32 [3], replicated, may hold values from -1 to 1, as said below
- across_kernels: bfloat16 [3, 128, 128], replicated, may hold values from -0.3125 to 0.3125
- across_offsets: int32 [3], replicated, may hold values from -1 to 1, as said below
- resp_start: int32 [13], replicated, may hold values from 0 to 21
- resp_values: bfloat16 [13, 20], replicated, may hold values from 0.049804688 to 0.3984375
Outputs:
- synthetic: float32 [13, 2048, 256], P(None, ('slab', 'line')), parts along dimension 1
- angles: float32 [2048, 256], P(('slab', 'line')), parts along dimension 0
There are 2 independent parts, one for each index of `slab`. A program takes and returns all parts, laid end to end along the dimension named above; an argument that names none is the same for every part. Nothing has to cross between parts.
Inputs may be any that keep to these rules, and one draw needn't show every extreme that they name: `along_offsets`: the three entries are -1, 0 and 1, each once. `across_offsets`: the three entries are -1, 0 and 1, each once.
All inputs are finite; a program needn't handle non-finite values.
Results may differ from a plain program's by a relative error of at most 0.0003.
Values may be sent and summed in bfloat16 or wider, within the bound.
A program may use at most 192 MiB of HBM per device.

v0:
```python
import jax
import jax.numpy as jnp
from jax import lax
from jax.sharding import PartitionSpec as P

BLK = 128
SPB = 10


def extended(shard, sides, width):
    for axis, dim in sides:
        size, length = (lax.axis_size(axis), shard.shape[dim])
        up = [(i, (i + 1) % size) for i in range(size - 1)]
        down = [(j, i) for i, j in up]
        last = lax.slice_in_dim(shard, length - width, length, axis=dim)
        leading = lax.slice_in_dim(shard, 0, width, axis=dim)
        before = lax.ppermute(last, axis, up)
        after = lax.ppermute(leading, axis, down)
        shard = jnp.concatenate([before, shard, after], axis=dim)
    return shard


def pick_kernels(kernels, offsets):
    shifts = jnp.arange(3, dtype=jnp.int32) - 1
    onehot = (offsets[None, :] == shifts[:, None]).astype(jnp.float32)
    return jnp.einsum(
        "sk,kpq->spq", onehot, kernels.astype(jnp.float32), precision=lax.Precision.HIGHEST
    )


def dense_response(resp_start, resp_values, band_total):
    bands = jnp.arange(band_total, dtype=jnp.int32)
    local = bands[None, :] - SPB * resp_start[:, None]
    slots = jnp.arange(2 * SPB, dtype=jnp.int32)
    hits = local[:, :, None] == slots[None, None, :]
    return jnp.sum(
        jnp.where(hits, resp_values.astype(jnp.float32)[:, None, :], jnp.float32(0.0)), axis=-1
    )


def along_blocks(padded, chosen, count):
    total = None
    for index in range(3):
        term = jnp.einsum(
            "pq,bnqc->bnpc",
            chosen[index],
            padded[:, index : index + count],
            precision=lax.Precision.HIGHEST,
        )
        total = term if total is None else total + term
    return total


def across_filter(field, chosen):
    count = field.shape[2] // BLK
    blocks = field.reshape(field.shape[0], field.shape[1], count, BLK)
    padded = jnp.pad(blocks, ((0, 0), (0, 0), (1, 1), (0, 0)))
    total = jnp.zeros(blocks.shape, jnp.float32)
    for index in range(3):
        total = total + jnp.einsum(
            "pq,blnq->blnp",
            chosen[index],
            padded[:, :, index : index + count],
            precision=lax.Precision.HIGHEST,
        )
    return total.reshape(field.shape)


def respond_plain(weights, field):
    return jnp.einsum(
        "mb,blc->mlc", weights.astype(jnp.bfloat16), field, preferred_element_type=jnp.float32
    )


def on_device(
    cube,
    observed,
    along_kernels,
    along_offsets,
    across_kernels,
    across_offsets,
    resp_start,
    resp_values,
):
    band_share = cube.shape[0]
    line_rows = cube.shape[1]
    column_count = cube.shape[2]
    band_total = band_share * lax.axis_size("band")
    along_pick = pick_kernels(along_kernels, along_offsets)
    across_pick = pick_kernels(across_kernels, across_offsets)
    response = dense_response(resp_start, resp_values, band_total)
    local_response = lax.dynamic_slice_in_dim(
        response, lax.axis_index("band") * band_share, band_share, 1
    )
    count = line_rows // BLK
    folded = respond_plain(local_response, cube)
    summed = lax.psum(folded, "band")
    padded_sum = extended(summed, (("line", 1),), BLK)
    padded = padded_sum.reshape(summed.shape[0], count + 2, BLK, column_count)
    smooth = along_blocks(padded, along_pick, count).reshape(summed.shape)
    partial_value = across_filter(smooth, across_pick)
    seen = observed.astype(jnp.float32)
    inner = jnp.sum(partial_value * seen, axis=0)
    first = jnp.sqrt(jnp.sum(partial_value * partial_value, axis=0))
    second = jnp.sqrt(jnp.sum(seen * seen, axis=0))
    angles = jnp.arccos(jnp.clip(inner / jnp.maximum(first * second, 1.0), -1.0, 1.0))
    return (partial_value, angles)


def solution(mesh):
    placed = (
        P("band", ("slab", "line"), None),
        P(None, ("slab", "line"), None),
        P(),
        P(),
        P(),
        P(),
        P(),
        P(),
    )
    return jax.shard_map(
        on_device,
        mesh=mesh,
        in_specs=placed,
        out_specs=(P(None, ("slab", "line"), None), P(("slab", "line"), None)),
        check_vma=False,
    )
```

profile of v0, /device:TPU:0, one launch (start us, length us, event | category | flops | bytes accessed | tf_op | source)
XLA Modules:
  0.0 157.4 jit_solution(8674825454620172075)
XLA Ops:
  7.2 0.0 copy-start
  7.2 0.0 all-reduce.3.cloned.1.call-start
  7.2 0.7 broadcast_multiply_fusion
  7.9 0.1 iota_subtract_fusion
  8.0 0.7 convert_element_type.8
  8.7 0.1 select_reduce_fusion
  8.8 8.8 %fusion = f32[13,128,256]{2,0,1:T(8,128)} fusion(bf16[115,128,256]{2,1,0:T(8,128)(2,1)} %param.8, bf16[13,230]{1,0:T(8,128)(2,1)S(1)} %select_reduce_fusion, s32[]{:T(128)S(6)} %select_n.8), kind=kOutput, calls=%fused_computation | convolution fusion | flops 97976320 | bytes 9244676 | tf_op jit(solution)/shard_map/mb,blc->mlc/dot_general | solution.py:70
  17.6 0.0 all-reduce.3.cloned.1.call-update
  17.6 0.0 copy-start.7
  17.6 0.0 copy-start.6
  17.6 0.0 copy-start.8
  17.6 24.1 %all-reduce.3.cloned.1.call-done = f32[13,128,256]{2,0,1:T(8,128)} async-done(((f32[13,128,256]{2,0,1:T(8,128)}), f32[13,128,256]{2,0,1:T(8,128)}) %all-reduce.3.cloned.1.call-update) | async-done | bytes 1703952 | tf_op jit(solution)/shard_map/psum | solution.py:97
  41.8 2.6 %copy.36 = f32[13,128,256]{2,1,0:T(8,128)S(1)} copy(f32[13,128,256]{2,0,1:T(8,128)} %all-reduce.3.cloned.1.call-done) | data formatting | bytes 3407872 | tf_op jit(solution)/shard_map/psum | solution.py:97
  44.4 3.8 %collective-permute-start = (f32[13,128,256]{2,1,0:T(8,128)S(1)}, f32[13,128,256]{2,1,0:T(8,128)S(1)}, u32[]{:S(2)}, u32[]{:S(2)}) collective-permute-start(f32[13,128,256]{2,1,0:T(8,128)S(1)} %copy.36), channel_id=1, source_target_pairs={{0,2},{2,4},{4,6},{6,8},{8,10},{10,12},{12,14},{1,3},{3,5},{5,7},{... | collective-permute-start | bytes 5111816 | tf_op jit(solution)/shard_map/ppermute | solution.py:17
  48.1 1.3 collective-permute-start.1
  49.4 0.0 copy-done
  49.4 0.0 copy-done.7
  49.5 0.3 fusion.14
  49.7 0.0 copy-done.6
  49.7 0.0 copy-done.8
  49.7 0.3 fusion.12
  50.0 0.1 fusion.29
  50.2 0.8 fusion.28
  50.9 70.5 %collective-permute-done = f32[13,128,256]{2,1,0:T(8,128)S(1)} collective-permute-done((f32[13,128,256]{2,1,0:T(8,128)S(1)}, f32[13,128,256]{2,1,0:T(8,128)S(1)}, u32[]{:S(2)}, u32[]{:S(2)}) %collective-permute-start) | collective-permute-done | bytes 1703968 | tf_op jit(solution)/shard_map/ppermute | solution.py:17
  121.4 1.0 copy.38
  122.4 0.0 collective-permute-done.1
  122.5 1.0 copy.39
  123.5 0.6 copy-done.1
  124.0 0.7 pad_maximum_fusion
  124.8 2.6 %fusion.27 = (f32[13,1,128,256]{3,0,2,1:T(8,128)S(1)}, f32[13,1,128,256]{3,0,2,1:T(8,128)}, f32[13,1,128,256]{3,0,2,1:T(8,128)}) fusion(f32[13,3,128,256]{3,0,2,1:T(8,128)S(1)} %bitcast.67), kind=kLoop, calls=%fused_computation.37 | loop fusion | bytes 10223616 | tf_op jit(solution)/shard_map/slice | solution.py:47
  127.4 2.9 %copy.55 = f32[13,1,128,256]{2,3,0,1:T(8,128)} copy(f32[13,1,128,256]{3,0,2,1:T(8,128)} %get-tuple-element.11) | data formatting | bytes 3407872
  130.3 2.8 %copy.56 = f32[13,1,128,256]{2,3,0,1:T(8,128)} copy(f32[13,1,128,256]{3,0,2,1:T(8,128)} %get-tuple-element.12) | data formatting | bytes 3407872
  133.1 1.8 %copy.54 = f32[13,1,128,256]{2,3,0,1:T(8,128)} copy(f32[13,1,128,256]{3,0,2,1:T(8,128)S(1)} %get-tuple-element.10) | data formatting | bytes 3407872
  134.8 3.1 %fusion.6 = f32[13,256,128]{2,1,0:T(8,128)S(1)} fusion(f32[128,128,1]{1,0,2:T(8,128)S(1)} %bitcast.75, f32[13,1,128,256]{2,3,0,1:T(8,128)} %copy.55), kind=kOutput, calls=%fused_computation.9 | convolution fusion | flops 654311424 | bytes 3473408 | tf_op jit(solution)/shard_map/pq,bnqc->bnpc/dot_general | solution.py:44
  138.0 0.0 copy-done.3
  138.0 0.0 copy-start.4
  138.0 1.6 %fusion.4 = f32[13,256,128]{2,1,0:T(8,128)S(1)} fusion(f32[128,128,1]{1,0,2:T(8,128)S(1)} %bitcast.74, f32[13,1,128,256]{2,3,0,1:T(8,128)S(1)} %copy-done.3), kind=kOutput, calls=%fused_computation.7 | convolution fusion | flops 654311424 | bytes 3473408 | tf_op jit(solution)/shard_map/pq,bnqc->bnpc/dot_general | solution.py:44
  139.6 1.6 %add_add_fusion.1 = f32[13,256,128]{2,1,0:T(8,128)S(1)} fusion(f32[13,256,128]{2,1,0:T(8,128)S(1)} %fusion.4, f32[13,256,128]{2,1,0:T(8,128)S(1)} %fusion.6, f32[128,128,1]{1,0,2:T(8,128)S(1)} %bitcast.71, f32[13,1,128,256]{2,3,0,1:T(8,128)S(1)} %copy-done.4), kind=kOutput, calls=%fused_computation.15 | convolution fusion | flops 655163392 | bytes 6881280 | tf_op jit(solution)/shard_map/pq,bnqc->bnpc/dot_general | solution.py:44
  141.2 1.6 %fusion.30 = f32[13,128,2,128]{1,3,2,0:T(8,128)S(1)} fusion(f32[13,128,2,128]{1,3,2,0:T(8,128)S(1)} %bitcast.64, f32[128,128,1,1]{1,0,3,2:T(8,128)S(1)} %bitcast.73), kind=kOutput, calls=%fused_computation.40 | convolution fusion | flops 654311424 | bytes 3473408 | tf_op jit(solution)/shard_map/pq,blnq->blnp/dot_general | solution.py:60
  142.8 0.0 copy-start.5
  142.9 1.5 fusion.31
  144.4 1.8 %multiply_reduce_fusion = (f32[128,2,128]{0,2,1:T(8,128)}, f32[13,128,2,128]{1,3,2,0:T(8,128)S(1)}) fusion(f32[13,128,2,128]{1,3,2,0:T(8,128)S(1)} %bitcast.66, f32[128,128,1,1]{1,0,3,2:T(8,128)S(1)} %bitcast.70, f32[13,128,2,128]{1,3,2,0:T(8,128)S(1)} %fusion.31, f32[13,128,2,128]{1,3,2,0:T(8,128)S(1)} %fusion.30), kind=kOutput, calls=%fused_computation.13 | convolution fusion | flops 328826880 | bytes 7012352 | tf_op jit(solution)/shard_map/pq,blnq->blnp/dot_general | solution.py:60
  146.1 0.7 copy.49
  146.9 0.0 copy-start.2
  146.9 1.1 sqrt.9
  148.0 0.1 copy.48
  148.1 1.5 fusion.3
  149.5 1.0 sqrt_atan2_fusion
  (6 shorter events, 0.0 us)
Async XLA Ops:
  7.2 42.3 %copy-start = (bf16[3,128,128]{2,1,0:T(8,128)(2,1)S(1)}, bf16[3,128,128]{2,1,0:T(8,128)(2,1)}, u32[]{:S(2)}) copy-start(bf16[3,128,128]{2,1,0:T(8,128)(2,1)} %param.10) | copy-start | bytes 294916
  7.2 34.6 %all-reduce.3.cloned.1.call-start = ((), (), s32[]{:S(2)}) async-start(), calls=%async_computation | async-start | bytes 4194304 | tf_op jit(solution)/shard_map/psum | solution.py:97
  17.6 31.8 %copy-start.7 = (s32[3]{0:T(128)S(1)}, s32[3]{0:T(128)}, u32[]{:S(2)}) copy-start(s32[3]{0:T(128)} %param.11) | copy-start | bytes 40
  17.6 32.1 %copy-start.6 = (bf16[3,128,128]{2,1,0:T(8,128)(2,1)S(1)}, bf16[3,128,128]{2,1,0:T(8,128)(2,1)}, u32[]{:S(2)}) copy-start(bf16[3,128,128]{2,1,0:T(8,128)(2,1)} %param.12) | copy-start | bytes 294916
  17.6 32.1 %copy-start.8 = (s32[3]{0:T(128)S(1)}, s32[3]{0:T(128)}, u32[]{:S(2)}) copy-start(s32[3]{0:T(128)} %param.13) | copy-start | bytes 40
  44.4 77.1 %collective-permute-start = (f32[13,128,256]{2,1,0:T(8,128)S(1)}, f32[13,128,256]{2,1,0:T(8,128)S(1)}, u32[]{:S(2)}, u32[]{:S(2)}) collective-permute-start(f32[13,128,256]{2,1,0:T(8,128)S(1)} %copy.36), channel_id=1, source_target_pairs={{0,2},{2,4},{4,6},{6,8},{8,10},{10,12},{12,14},{1,3},{3,5},{5,7},{... | collective-permute-start | bytes 5111816 | tf_op jit(solution)/shard_map/ppermute | solution.py:17
  48.1 74.3 %collective-permute-start.1 = (f32[13,128,256]{2,1,0:T(8,128)S(1)}, f32[13,128,256]{2,1,0:T(8,128)S(1)}, u32[]{:S(2)}, u32[]{:S(2)}) collective-permute-start(f32[13,128,256]{2,1,0:T(8,128)S(1)} %copy.36), channel_id=1, source_target_pairs={{2,0},{4,2},{6,4},{8,6},{10,8},{12,10},{14,12},{3,1},{5,3},{7,5},{... | collective-permute-start | bytes 5111816 | tf_op jit(solution)/shard_map/ppermute | solution.py:18
  122.4 1.6 %copy-start.1 = (f32[13,128,256]{2,0,1:T(8,128)S(1)}, f32[13,128,256]{2,0,1:T(8,128)}, u32[]{:S(2)}) copy-start(f32[13,128,256]{2,0,1:T(8,128)} %all-reduce.3.cloned.1.call-done) | copy-start | bytes 5111812
  134.8 3.1 %copy-start.3 = (f32[13,1,128,256]{2,3,0,1:T(8,128)S(1)}, f32[13,1,128,256]{2,3,0,1:T(8,128)}, u32[]{:S(2)}) copy-start(f32[13,1,128,256]{2,3,0,1:T(8,128)} %copy.56) | copy-start | bytes 5111812
  138.0 1.6 %copy-start.4 = (f32[13,1,128,256]{2,3,0,1:T(8,128)S(1)}, f32[13,1,128,256]{2,3,0,1:T(8,128)}, u32[]{:S(2)}) copy-start(f32[13,1,128,256]{2,3,0,1:T(8,128)} %copy.54) | copy-start | bytes 5111812
  142.8 1.5 copy-start.5
  146.9 3.6 %copy-start.2 = (f32[13,128,256]{2,1,0:T(8,128)}, f32[13,128,256]{2,1,0:T(8,128)S(1)}, u32[]{:S(2)}) copy-start(f32[13,128,256]{2,1,0:T(8,128)S(1)} %copy.49) | copy-start | bytes 5111812
Sparse Core Ops, SparseCore 0:
  17.7 24.0 all-reduce.2
where the time goes:
time: 158 us; the launch traced here: 157 us
  waiting for transfers between devices  94.6 us (60%)
  matrix products  20.5 us (13%)
  local copies, waits for them, and re-layouts  18.1 us (11%)
  between operations  14.3 us (9%)
  starting transfers between devices  5.09 us (3%)
  other arithmetic  4.75 us (3%)
    ppermute x1, waiting for transfers between devices, extended(): before = lax.ppermute(last, axis, up)  70.5 us
    psum x1, waiting for transfers between devices, on_device(): summed = lax.psum(folded, 'band')  24.1 us
    dot_general x1, matrix products, respond_plain(): jnp.einsum('mb,blc->mlc', weights.astype(jnp.bfloat16), field, preferred_...  8.77 us
    unnamed x22, local copies, waits for them, and re-layouts  8.75 us
    dot_general x3, matrix products, along_blocks(): jnp.einsum('pq,bnqc->bnpc', chosen[index], padded[:, index:index + count]...  6.31 us
    dot_general x3, matrix products, across_filter(): jnp.einsum('pq,blnq->blnp', chosen[index], padded[:, :, index:index + cou...  4.89 us
    ppermute x1, starting transfers between devices, extended(): before = lax.ppermute(last, axis, up)  3.76 us
  transfers between devices with their start and end apart: 3, of which 2 were waited for; matrix products, arithmetic and copies ran while one was open for 2% of the time, Pallas kernels for 0%

commit v1 on v0

--- a/solution.py
+++ b/solution.py
@@ -94,7 +94,8 @@
     )
     count = line_rows // BLK
     folded = respond_plain(local_response, cube)
-    summed = lax.psum(folded, "band")
+    parts = lax.all_gather(folded, "band", axis=0, tiled=False)
+    summed = parts.sum(axis=0)
     padded_sum = extended(summed, (("line", 1),), BLK)
     padded = padded_sum.reshape(summed.shape[0], count + 2, BLK, column_count)
     smooth = along_blocks(padded, along_pick, count).reshape(summed.shape)

time: 158 us -> 140 us (0.89)
  local copies, waits for them, and re-layouts: 18.1 us -> 4.4 us
  waiting for transfers between devices: 94.6 us -> 86.3 us
  other arithmetic: 4.75 us -> 6.76 us
    psum x1 -> x0, waiting for transfers between devices: 24.1 us -> none  [on_device(): summed = lax.psum(folded, 'band')]
    all_gather x0 -> x1, waiting for transfers between devices: none -> 15.4 us  [on_device(): parts = lax.all_gather(folded, 'band', axis=0, tiled=False)]
    unnamed x22 -> x11, local copies, waits for them, and re-layouts: 8.75 us -> 0.77 us
    slice x1 -> x0, local copies, waits for them, and re-layouts: 2.65 us -> none  [along_blocks(): padded[:, index:index + count]]
    psum x1 -> x0, local copies, waits for them, and re-layouts: 2.58 us -> none  [on_device(): summed = lax.psum(folded, 'band')]
    reduce_sum x0 -> x1, other arithmetic: none -> 2.4 us  [on_device(): summed = parts.sum(axis=0)]
    dot_general x3, matrix products: 6.31 us -> 8.65 us  [along_blocks(): jnp.einsum('pq,bnqc->bnpc', chosen[index], padded[:, index:index + count]...]
    dot_general x0 -> x1, local copies, waits for them, and re-layouts: none -> 2.18 us  [respond_plain(): jnp.einsum('mb,blc->mlc', weights.astype(jnp.bfloat16), field, preferred_...]
  transfers between devices with their start and end apart: 3 -> 3, of which waited for: 2 -> 2; matrix products, arithmetic and copies ran while one was open for 2% -> 1% of each run, Pallas kernels for 0% -> 0%
where the time goes in v1:
time: 140 us; the launch traced here: 139 us
  waiting for transfers between devices  86.3 us (62%)
  matrix products  21.8 us (16%)
  between operations  14.2 us (10%)
  other arithmetic  6.76 us (5%)
  starting transfers between devices  5.27 us (4%)
  local copies, waits for them, and re-layouts  4.4 us (3%)
    ppermute x1, waiting for transfers between devices, extended(): before = lax.ppermute(last, axis, up)  70.9 us
    all_gather x1, waiting for transfers between devices, on_device(): parts = lax.all_gather(folded, 'band', axis=0, tiled=False)  15.4 us
    dot_general x3, matrix products, along_blocks(): jnp.einsum('pq,bnqc->bnpc', chosen[index], padded[:, index:index + count]...  8.65 us
    dot_general x1, matrix products, respond_plain(): jnp.einsum('mb,blc->mlc', weights.astype(jnp.bfloat16), field, preferred_...  7.46 us
    dot_general x3, matrix products, across_filter(): jnp.einsum('pq,blnq->blnp', chosen[index], padded[:, :, index:index + cou...  5.13 us
    ppermute x1, starting transfers between devices, extended(): before = lax.ppermute(last, axis, up)  3.75 us
  transfers between devices with their start and end apart: 3, of which 2 were waited for; matrix products, arithmetic and copies ran while one was open for 1% of the time, Pallas kernels for 0%

profile of v1, /device:TPU:0, one launch (start us, length us, event | category | flops | bytes accessed | tf_op | source)
XLA Modules:
  0.0 138.8 jit_solution(430036859707887252)
XLA Ops:
  7.2 0.0 copy-start
  7.2 0.0 all-gather.3.cloned.1.call-start
  7.2 0.7 broadcast_multiply_fusion
  7.9 0.1 iota_subtract_fusion
  8.0 0.7 convert_element_type.8
  8.7 0.1 select_reduce_fusion
  8.8 7.5 %fusion = f32[13,128,256]{2,0,1:T(8,128)S(1)} fusion(bf16[115,128,256]{2,1,0:T(8,128)(2,1)} %param.8, bf16[13,230]{1,0:T(8,128)(2,1)S(1)} %select_reduce_fusion, s32[]{:T(128)S(6)} %select_n.8), kind=kOutput, calls=%fused_computation | convolution fusion | flops 97976320 | bytes 9244676 | tf_op jit(solution)/shard_map/mb,blc->mlc/dot_general | solution.py:70
  16.3 2.2 %copy.41 = f32[13,128,256]{2,1,0:T(8,128)} copy(f32[13,128,256]{2,0,1:T(8,128)S(1)} %fusion) | data formatting | bytes 3407872 | tf_op jit(solution)/shard_map/mb,blc->mlc/dot_general | solution.py:70
  18.4 0.0 all-gather.3.cloned.1.call-update
  18.5 15.4 %all-gather.3.cloned.1.call-done = f32[26,128,256]{2,1,0:T(8,128)} async-done(((f32[13,128,256]{2,1,0:T(8,128)}), f32[26,128,256]{2,1,0:T(8,128)}) %all-gather.3.cloned.1.call-update) | async-done | bytes 3407888 | tf_op jit(solution)/shard_map/all_gather | solution.py:97
  33.9 0.0 copy-start.3
  33.9 0.0 copy-start.2
  33.9 0.0 copy-start.4
  33.9 2.4 %reduce_sum.46 = f32[13,128,256]{2,1,0:T(8,128)S(1)} reduce(f32[2,13,128,256]{3,2,1,0:T(8,128)} %bitcast.75, f32[]{:T(128)} %constant.10.clone.1), dimensions={0}, to_apply=%region_1.2 | reduce | flops 425984 | bytes 5111812 | tf_op jit(solution)/shard_map/reduce_sum | solution.py:98
  36.3 3.8 %collective-permute-start = (f32[13,128,256]{2,1,0:T(8,128)S(1)}, f32[13,128,256]{2,1,0:T(8,128)S(1)}, u32[]{:S(2)}, u32[]{:S(2)}) collective-permute-start(f32[13,128,256]{2,1,0:T(8,128)S(1)} %reduce_sum.46), channel_id=1, source_target_pairs={{0,2},{2,4},{4,6},{6,8},{8,10},{10,12},{12,14},{1,3},{3,5},{5,7},{... | collective-permute-start | bytes 5111816 | tf_op jit(solution)/shard_map/ppermute | solution.py:17
  40.0 1.5 %collective-permute-start.1 = (f32[13,128,256]{2,1,0:T(8,128)S(1)}, f32[13,128,256]{2,1,0:T(8,128)S(1)}, u32[]{:S(2)}, u32[]{:S(2)}) collective-permute-start(f32[13,128,256]{2,1,0:T(8,128)S(1)} %reduce_sum.46), channel_id=1, source_target_pairs={{2,0},{4,2},{6,4},{8,6},{10,8},{12,10},{14,12},{3,1},{5,3},{7,5},{... | collective-permute-start | bytes 5111816 | tf_op jit(solution)/shard_map/ppermute | solution.py:18
  41.5 0.0 copy-done
  41.5 0.0 copy-done.3
  41.5 0.3 fusion.9
  41.8 0.0 copy-done.2
  41.8 0.0 copy-done.4
  41.8 0.3 fusion.7
  42.1 0.1 fusion.23
  42.3 0.1 fusion.22
  42.4 70.9 %collective-permute-done = f32[13,128,256]{2,1,0:T(8,128)S(1)} collective-permute-done((f32[13,128,256]{2,1,0:T(8,128)S(1)}, f32[13,128,256]{2,1,0:T(8,128)S(1)}, u32[]{:S(2)}, u32[]{:S(2)}) %collective-permute-start) | collective-permute-done | bytes 1703968 | tf_op jit(solution)/shard_map/ppermute | solution.py:17
  113.3 0.0 collective-permute-done.1
  113.3 0.3 pad_maximum_fusion
  113.7 2.9 %fusion.5 = f32[13,256,128]{2,1,0:T(8,128)S(1)} fusion(f32[128,128,1]{1,0,2:T(8,128)S(1)} %bitcast.82, f32[13,3,128,256]{3,2,1,0:T(8,128)S(1)} %bitcast.71), kind=kOutput, calls=%fused_computation.10 | convolution fusion | flops 654311424 | bytes 3473408 | tf_op jit(solution)/shard_map/pq,bnqc->bnpc/dot_general | solution.py:44
  116.6 2.9 %fusion.6 = f32[13,256,128]{2,1,0:T(8,128)S(1)} fusion(f32[128,128,1]{1,0,2:T(8,128)S(1)} %bitcast.81, f32[13,3,128,256]{3,2,1,0:T(8,128)S(1)} %bitcast.72), kind=kOutput, calls=%fused_computation.12 | convolution fusion | flops 654311424 | bytes 3473408 | tf_op jit(solution)/shard_map/pq,bnqc->bnpc/dot_general | solution.py:44
  119.5 2.9 %add_add_fusion.1 = f32[13,256,128]{2,1,0:T(8,128)S(1)} fusion(f32[13,256,128]{2,1,0:T(8,128)S(1)} %fusion.6, f32[13,256,128]{2,1,0:T(8,128)S(1)} %fusion.5, f32[128,128,1]{1,0,2:T(8,128)S(1)} %bitcast.78, f32[13,3,128,256]{3,2,1,0:T(8,128)S(1)} %bitcast.73), kind=kOutput, calls=%fused_computation.15 | convolution fusion | flops 655163392 | bytes 6881280 | tf_op jit(solution)/shard_map/pq,bnqc->bnpc/dot_general | solution.py:44
  122.4 1.6 %fusion.24 = f32[13,128,2,128]{1,3,2,0:T(8,128)S(1)} fusion(f32[13,128,2,128]{1,3,2,0:T(8,128)S(1)} %bitcast.68, f32[128,128,1,1]{1,0,3,2:T(8,128)S(1)} %bitcast.80), kind=kOutput, calls=%fused_computation.39 | convolution fusion | flops 654311424 | bytes 3473408 | tf_op jit(solution)/shard_map/pq,blnq->blnp/dot_general | solution.py:60
  124.0 1.7 %fusion.25 = f32[13,128,2,128]{1,3,2,0:T(8,128)S(1)} fusion(f32[13,128,2,128]{1,3,2,0:T(8,128)S(1)} %bitcast.69, f32[128,128,1,1]{1,0,3,2:T(8,128)S(1)} %bitcast.79), kind=kOutput, calls=%fused_computation.40 | convolution fusion | flops 327155712 | bytes 3473408 | tf_op jit(solution)/shard_map/pq,blnq->blnp/dot_general | solution.py:60
  125.7 1.8 %multiply_reduce_fusion = (f32[128,2,128]{0,2,1:T(8,128)}, f32[13,128,2,128]{1,3,2,0:T(8,128)S(1)}) fusion(f32[13,128,2,128]{1,3,2,0:T(8,128)S(1)} %bitcast.70, f32[128,128,1,1]{1,0,3,2:T(8,128)S(1)} %bitcast.77, f32[13,128,2,128]{1,3,2,0:T(8,128)S(1)} %fusion.25, f32[13,128,2,128]{1,3,2,0:T(8,128)S(1)} %fusion.24), kind=kOutput, calls=%fused_computation.13 | convolution fusion | flops 328826880 | bytes 7012352 | tf_op jit(solution)/shard_map/pq,blnq->blnp/dot_general | solution.py:60
  127.5 0.7 copy.51
  128.3 0.0 copy-start.1
  128.3 1.1 sqrt.9
  129.4 0.1 copy.50
  129.5 1.5 %fusion.3 = (f32[128,256]{1,0:T(8,128)S(1)}, f32[128,256]{1,0:T(8,128)S(1)}) fusion(bf16[13,128,256]{2,1,0:T(8,128)(2,1)} %param.9, f32[13,128,256]{2,1,0:T(8,128)S(1)} %copy.51), kind=kLoop, calls=%fused_computation.6 | loop fusion | flops 2064384 | bytes 2818048 | tf_op jit(solution)/shard_map/reduce_sum | solution.py:106
  130.9 1.0 sqrt_atan2_fusion
  131.9 0.0 copy-done.1
  (1 shorter events, 0.0 us)
Async XLA Ops:
  7.2 34.4 %copy-start = (bf16[3,128,128]{2,1,0:T(8,128)(2,1)S(1)}, bf16[3,128,128]{2,1,0:T(8,128)(2,1)}, u32[]{:S(2)}) copy-start(bf16[3,128,128]{2,1,0:T(8,128)(2,1)} %param.10) | copy-start | bytes 294916
  7.2 26.7 %all-gather.3.cloned.1.call-start = ((), (), s32[]{:S(2)}) async-start(), calls=%async_computation | async-start | bytes 5111808 | tf_op jit(solution)/shard_map/all_gather | solution.py:97
  33.9 7.7 %copy-start.3 = (s32[3]{0:T(128)S(1)}, s32[3]{0:T(128)}, u32[]{:S(2)}) copy-start(s32[3]{0:T(128)} %param.11) | copy-start | bytes 40
  33.9 8.0 %copy-start.2 = (bf16[3,128,128]{2,1,0:T(8,128)(2,1)S(1)}, bf16[3,128,128]{2,1,0:T(8,128)(2,1)}, u32[]{:S(2)}) copy-start(bf16[3,128,128]{2,1,0:T(8,128)(2,1)} %param.12) | copy-start | bytes 294916
  33.9 8.0 %copy-start.4 = (s32[3]{0:T(128)S(1)}, s32[3]{0:T(128)}, u32[]{:S(2)}) copy-start(s32[3]{0:T(128)} %param.13) | copy-start | bytes 40
  36.3 77.1 %collective-permute-start = (f32[13,128,256]{2,1,0:T(8,128)S(1)}, f32[13,128,256]{2,1,0:T(8,128)S(1)}, u32[]{:S(2)}, u32[]{:S(2)}) collective-permute-start(f32[13,128,256]{2,1,0:T(8,128)S(1)} %reduce_sum.46), channel_id=1, source_target_pairs={{0,2},{2,4},{4,6},{6,8},{8,10},{10,12},{12,14},{1,3},{3,5},{5,7},{... | collective-permute-start | bytes 5111816 | tf_op jit(solution)/shard_map/ppermute | solution.py:17
  40.0 73.3 %collective-permute-start.1 = (f32[13,128,256]{2,1,0:T(8,128)S(1)}, f32[13,128,256]{2,1,0:T(8,128)S(1)}, u32[]{:S(2)}, u32[]{:S(2)}) collective-permute-start(f32[13,128,256]{2,1,0:T(8,128)S(1)} %reduce_sum.46), channel_id=1, source_target_pairs={{2,0},{4,2},{6,4},{8,6},{10,8},{12,10},{14,12},{3,1},{5,3},{7,5},{... | collective-permute-start | bytes 5111816 | tf_op jit(solution)/shard_map/ppermute | solution.py:18
  128.3 3.6 %copy-start.1 = (f32[13,128,256]{2,1,0:T(8,128)}, f32[13,128,256]{2,1,0:T(8,128)S(1)}, u32[]{:S(2)}) copy-start(f32[13,128,256]{2,1,0:T(8,128)S(1)} %copy.51) | copy-start | bytes 5111812
Sparse Core Ops, SparseCore 0:
  18.6 15.2 all-gather.2
